TPU v7x, 256 devices: a whole 4x4x8 slice. The times are simulated.
256 devices in a mesh: row: 16 (over x, z_hi), col: 16 (over y, z_lo, core).
Axes of the slice: x: 4, y: 4, z: 8 (z_hi: 4, z_lo: 2; z = z_hi * 2 + z_lo), core: 2. Of those that a mesh axis runs over, the one named last changes fastest.
Arguments:
- tile_count: int32 [16, 16], P('row', 'col'), may hold values from 1 to 40, as said below
- tile_rows: int32 [16, 16, 40], P('row', 'col'), may hold values from 0 to 31, as said below
- tile_cols: int32 [16, 16, 40], P('row', 'col'), may hold values from 0 to 31, as said below
- tiles: float32 [16, 16, 40, 256, 256], P('row', 'col')
- block: float32 [64, 131072], P(None, ('row', 'col')), may hold values from -6 to 6
Outputs:
- image_x: float32 [64, 131072], P(None, ('row', 'col'))
- image_w: float32 [64, 131072], P(None, ('row', 'col'))
- grams: float32 [4, 64, 64], replicated
Inputs may be any that keep to these rules, and one draw needn't show every extreme that they name: `tile_count`: live slots of each grid block; the largest count over the grid is exactly 40. `tile_rows`: live slots of one grid block hold distinct positions whose global tile row is at least the global tile column; slots at or past the count hold 0. `tile_cols`: paired with tile_rows as above; slots at or past the count hold 0.
All inputs are finite; a program needn't handle non-finite values.
Results may differ from a plain program's by a relative error of at most 0.0001.
Values sent between devices are 32-bit elements; how exact they have to be, the bound alone decides.
A program may use at most 64 MiB of HBM per device.

v0:
```python
import jax
import jax.numpy as jnp
from jax import lax
from jax.sharding import PartitionSpec as P

highest = lax.Precision.HIGHEST


def passed_along(array, axis, by):
    size = lax.axis_size(axis)
    return lax.ppermute(array, axis, [(i, (i + by) % size) for i in range(size)])


def inner_prod(left, right):
    return lax.dot_general(
        left, right, (((1,), (1,)), ((), ())), precision=highest, preferred_element_type=jnp.float32
    )


def on_device(tile_count, tile_rows, tile_cols, tiles, block):
    vec_count, seg_rows = block.shape
    tile_size = tiles.shape[-1]
    seg_tiles = seg_rows // tile_size
    grid_rows = lax.axis_size("row")
    grid_cols = lax.axis_size("col")
    total_rows = seg_rows * grid_rows * grid_cols
    live_count = tile_count[0, 0]
    row_ids = tile_rows[0, 0]
    col_ids = tile_cols[0, 0]
    tile_data = tiles[0, 0]
    row_slots = grid_cols * seg_tiles
    col_slots = grid_rows * seg_tiles

    def expand(vectors):
        near_vec = lax.all_gather(vectors, "col", axis=1, tiled=True)
        far_vec = lax.all_gather(vectors, "row", axis=1, tiled=True)
        near_tiles = near_vec.reshape(vec_count, row_slots, tile_size)
        far_tiles = far_vec.reshape(vec_count, col_slots, tile_size)
        groups = (live_count + 7) // 8

        def accumulate(counter, carry):
            sums_rows, sums_cols = carry
            offset = counter * 8
            block_tiles = lax.dynamic_slice_in_dim(tile_data, offset, 8, 0)
            slot_rows = lax.dynamic_slice_in_dim(row_ids, offset, 8, 0)
            slot_cols = lax.dynamic_slice_in_dim(col_ids, offset, 8, 0)
            live_mask = (offset + jnp.arange(8, dtype=jnp.int32) < live_count).astype(jnp.float32)
            rows_in = jnp.take(near_tiles, slot_rows, axis=1)
            cols_in = jnp.take(far_tiles, slot_cols, axis=1)
            lower_part = (
                jnp.einsum("sij,ksj->ksi", block_tiles, cols_in, precision=highest)
                * live_mask[None, :, None]
            )
            upper_part = (
                jnp.einsum("sij,ksi->ksj", block_tiles, rows_in, precision=highest)
                * live_mask[None, :, None]
            )
            row_pick = (
                slot_rows[:, None] == jnp.arange(row_slots, dtype=jnp.int32)[None, :]
            ).astype(jnp.float32)
            col_pick = (
                slot_cols[:, None] == jnp.arange(col_slots, dtype=jnp.int32)[None, :]
            ).astype(jnp.float32)
            sums_rows = sums_rows + jnp.einsum(
                "ksi,sp->kpi", lower_part, row_pick, precision=highest
            )
            sums_cols = sums_cols + jnp.einsum(
                "ksi,sp->kpi", upper_part, col_pick, precision=highest
            )
            return (sums_rows, sums_cols)

        empty_rows = jnp.zeros((vec_count, row_slots, tile_size), jnp.float32)
        empty_cols = jnp.zeros((vec_count, col_slots, tile_size), jnp.float32)
        part_rows, part_cols = lax.fori_loop(0, groups, accumulate, (empty_rows, empty_cols))
        return (
            near_vec,
            far_vec,
            part_rows.reshape(vec_count, row_slots * tile_size),
            part_cols.reshape(vec_count, col_slots * tile_size),
        )

    def combine_sums(part_rows, part_cols):
        pieces_rows = part_rows.reshape(vec_count, grid_cols, seg_rows)
        pieces_cols = part_cols.reshape(vec_count, grid_rows, seg_rows)
        my_col = lax.axis_index("col")
        my_row = lax.axis_index("row")

        def select_piece(pieces, position):
            return lax.dynamic_index_in_dim(pieces, position, 1, keepdims=False)

        def pass_along_rows(counter, running):
            moved = passed_along(running, "col", 1)
            return moved + select_piece(
                pieces_rows, (my_col + 2 * grid_cols - 1 - counter) % grid_cols
            )

        def pass_along_cols(counter, running):
            moved = passed_along(running, "row", 1)
            return moved + select_piece(
                pieces_cols, (my_row + 2 * grid_rows - 1 - counter) % grid_rows
            )

        first_rows = select_piece(pieces_rows, (my_col + grid_cols - 1) % grid_cols)
        first_cols = select_piece(pieces_cols, (my_row + grid_rows - 1) % grid_rows)
        own_rows = lax.fori_loop(1, grid_cols, pass_along_rows, first_rows)
        own_cols = lax.fori_loop(1, grid_rows, pass_along_cols, first_cols)
        return own_rows + own_cols

    near_x, far_x, rows_x, cols_x = expand(block)
    image_x = combine_sums(rows_x, cols_x)
    first_term = inner_prod(block, image_x)
    rayleigh = lax.psum(first_term, ("row", "col")) / total_rows
    resid = image_x - jnp.dot(
        rayleigh, block, precision=highest, preferred_element_type=jnp.float32
    )
    near_w, far_w, rows_w, cols_w = expand(resid)
    image_w = combine_sums(rows_w, cols_w)
    cross_term = inner_prod(block, image_w)
    resid_term = inner_prod(resid, image_w)
    square_term = inner_prod(resid, resid)
    others = lax.psum(jnp.stack([cross_term, resid_term, square_term]), ("row", "col")) / total_rows
    grams = jnp.concatenate([rayleigh[None], others], axis=0)
    return (image_x, image_w, grams)


def solution(mesh):
    return jax.shard_map(
        on_device,
        mesh=mesh,
        in_specs=(
            P("row", "col"),
            P("row", "col", None),
            P("row", "col", None),
            P("row", "col", None, None, None),
            P(None, ("row", "col")),
        ),
        out_specs=(P(None, ("row", "col")), P(None, ("row", "col")), P()),
        check_vma=False,
    )
```

profile of v0, /device:TPU:1, one launch (start us, length us, event | category | flops | bytes accessed | tf_op | source)
XLA Modules:
  0.0 1077.0 jit_solution(5392531176664811493)
XLA Ops:
  9.4 40.8 %all-gather.7.cloned.1.call-done = f32[64,8192]{1,0:T(8,128)} async-done(((f32[64,512]{1,0:T(8,128)}), f32[64,8192]{1,0:T(8,128)}) %all-gather.7.cloned.1.call-update) | async-done | bytes 2097168 | tf_op jit(solution)/shard_map/all_gather | solution.py:35
  53.4 56.9 %all-gather.5.cloned.1.call-done = f32[64,8192]{1,0:T(8,128)} async-done(((f32[64,512]{1,0:T(8,128)}), f32[64,8192]{1,0:T(8,128)}) %all-gather.5.cloned.1.call-update) | async-done | bytes 2097168 | tf_op jit(solution)/shard_map/all_gather | solution.py:36
  115.4 17.8 %while.84 = (s32[]{:T(128)}, f32[64,32,256]{2,1,0:T(8,128)S(1)}, f32[64,32,256]{2,1,0:T(8,128)}, s32[]{:T(128)}, s32[40]{0:T(128)S(1)}, /*index=5*/s32[40]{0:T(1...) while((s32[]{:T(128)}, f32[64,32,256]{2,1,0:T(8,128)S(1)}, ...), condition=%wide.region_1.3_spmd, body=%wide.region_0.2_spmd.sunk | while | flops 907545280 | bytes 17834760 | solution.py:74
  140.4 217.7 %while.86 = (s32[]{:T(128)}, f32[64,512]{1,0:T(8,128)S(1)}, s32[]{:T(128)}, f32[64,16,512]{2,1,0:T(8,128)}, s32[]{:T(128)}, /*index=5*/s32[]{:T(128)}, s32[]{:T(128)}, s32[]{:T(128)}) while((s32[]{:T(128)}, f32[64,512]{1,0:T(8,128)S(1)}, s32[]{:T(128)}, f32[64,16,512]{2,1,0:T(8,128)}, s32[]{:T(128)}, /*index=5*/s32[]{:T(128)}, s32[]{:T(128)}, ...), condition=%wide.region_5.7_spmd, body=%wide.region_4.6_spmd.sunk | while | flops 32785 | bytes 1179932 | solution.py:106
  143.3 75.8 %collective-permute-done.1 = f32[64,512]{1,0:T(8,128)S(1)} collective-permute-done((f32[64,512]{1,0:T(8,128)S(1)}, f32[64,512]{1,0:T(8,128)S(1)}, u32[]{:S(2)}, u32[]{:S(2)}) %collective-permute-start.1) | collective-permute-done | bytes 131104 | tf_op jit(solution)/shard_map/while/body/eval_jaxpr/ppermute | solution.py:11
  245.8 9.6 collective-permute-done.1
  286.9 10.8 %collective-permute-done.1 = f32[64,512]{1,0:T(8,128)S(1)} collective-permute-done((f32[64,512]{1,0:T(8,128)S(1)}, f32[64,512]{1,0:T(8,128)S(1)}, u32[]{:S(2)}, u32[]{:S(2)}) %collective-permute-start.1) | collective-permute-done | bytes 131104 | tf_op jit(solution)/shard_map/while/body/eval_jaxpr/ppermute | solution.py:11
  299.2 9.9 collective-permute-done.1
  320.8 10.4 collective-permute-done.1
  358.1 108.0 %while.85 = (s32[]{:T(128)}, f32[64,512]{1,0:T(8,128)S(1)}, s32[]{:T(128)}, f32[64,16,512]{2,1,0:T(8,128)}, s32[]{:T(128)}, /*index=5*/s32[]{:T(128)}, s32[]{:T(128)}, s32[]{:T(128)}) while((s32[]{:T(128)}, f32[64,512]{1,0:T(8,128)S(1)}, s32[]{:T(128)}, f32[64,16,512]{2,1,0:T(8,128)}, s32[]{:T(128)}, /*index=5*/s32[]{:T(128)}, s32[]{:T(128)}, ...), condition=%wide.region_3.5_spmd, body=%wide.region_2.4_spmd.sunk | while | flops 32785 | bytes 1179932 | solution.py:105
  466.4 76.2 %psum.14 = f32[64,64]{0,1:T(8,128)S(1)} all-reduce(f32[64,64]{0,1:T(8,128)S(1)} %convolution_bitcast_fusion.3), channel_id=1, replica_groups=mesh['row'=16,'col'=16] {'row','col'}, use_global_device_ids=true, to_apply=%region_6.8 | all-reduce | flops 4096 | bytes 32768 | tf_op jit(solution)/shard_map/psum | solution.py:112
  545.5 30.2 %all-gather.11.cloned.1.call-done = f32[64,8192]{1,0:T(8,128)} async-done(((f32[64,512]{1,0:T(8,128)}), f32[64,8192]{1,0:T(8,128)}) %all-gather.11.cloned.1.call-update) | async-done | bytes 2097168 | tf_op jit(solution)/shard_map/all_gather | solution.py:35
  578.9 57.3 %all-gather.9.cloned.1.call-done = f32[64,8192]{1,0:T(8,128)} async-done(((f32[64,512]{1,0:T(8,128)}), f32[64,8192]{1,0:T(8,128)}) %all-gather.9.cloned.1.call-update) | async-done | bytes 2097168 | tf_op jit(solution)/shard_map/all_gather | solution.py:36
  641.3 17.8 %while.87 = (s32[]{:T(128)}, f32[64,32,256]{2,1,0:T(8,128)S(1)}, f32[64,32,256]{2,1,0:T(8,128)}, s32[]{:T(128)}, s32[40]{0:T(128)S(1)}, /*index=5*/s32[40]{0:T(1...) while((s32[]{:T(128)}, f32[64,32,256]{2,1,0:T(8,128)S(1)}, ...), condition=%wide.region_8.10_spmd, body=%wide.region_7.9_spmd.sunk | while | flops 907545280 | bytes 17834760 | solution.py:74
  666.3 222.1 %while.89 = (s32[]{:T(128)}, f32[64,512]{1,0:T(8,128)S(1)}, s32[]{:T(128)}, f32[64,16,512]{2,1,0:T(8,128)}, s32[]{:T(128)}, /*index=5*/s32[]{:T(128)}, s32[]{:T(128)}, s32[]{:T(128)}) while((s32[]{:T(128)}, f32[64,512]{1,0:T(8,128)S(1)}, s32[]{:T(128)}, f32[64,16,512]{2,1,0:T(8,128)}, s32[]{:T(128)}, /*index=5*/s32[]{:T(128)}, s32[]{:T(128)}, ...), condition=%wide.region_12.14_spmd, body=%wide.region_11.13_spmd.sunk | while | flops 32785 | bytes 1179932 | solution.py:106
  669.2 75.8 %collective-permute-done.3 = f32[64,512]{1,0:T(8,128)S(1)} collective-permute-done((f32[64,512]{1,0:T(8,128)S(1)}, f32[64,512]{1,0:T(8,128)S(1)}, u32[]{:S(2)}, u32[]{:S(2)}) %collective-permute-start.3) | collective-permute-done | bytes 131104 | tf_op jit(solution)/shard_map/while/body/eval_jaxpr/ppermute | solution.py:11
  771.8 9.6 collective-permute-done.3
  791.8 9.2 collective-permute-done.3
  812.7 10.7 collective-permute-done.3
  824.8 10.1 collective-permute-done.3
  846.6 10.4 collective-permute-done.3
  868.7 9.3 collective-permute-done.3
  888.4 104.1 %while.88 = (s32[]{:T(128)}, f32[64,512]{1,0:T(8,128)S(1)}, s32[]{:T(128)}, f32[64,16,512]{2,1,0:T(8,128)}, s32[]{:T(128)}, /*index=5*/s32[]{:T(128)}, s32[]{:T(128)}, s32[]{:T(128)}) while((s32[]{:T(128)}, f32[64,512]{1,0:T(8,128)S(1)}, s32[]{:T(128)}, f32[64,16,512]{2,1,0:T(8,128)}, s32[]{:T(128)}, /*index=5*/s32[]{:T(128)}, s32[]{:T(128)}, ...), condition=%wide.region_10.12_spmd, body=%wide.region_9.11_spmd.sunk | while | flops 32785 | bytes 1179932 | solution.py:105
  993.1 76.6 %psum.15 = f32[3,64,64]{1,2,0:T(8,128)S(1)} all-reduce(f32[3,64,64]{1,2,0:T(8,128)S(1)} %pad_maximum_fusion.1), channel_id=1, replica_groups=mesh['row'=16,'col'=16] {'row','col'}, use_global_device_ids=true, to_apply=%region_13.15 | all-reduce | flops 12288 | bytes 98304 | tf_op jit(solution)/shard_map/psum | solution.py:121
  (304 shorter events, 469.5 us)
Async XLA Ops:
  7.2 43.1 %all-gather.7.cloned.1.call-start = ((), (), s32[]{:S(2)}) async-start(), calls=%async_computation.1 | async-start | bytes 2228224 | tf_op jit(solution)/shard_map/all_gather | solution.py:35
  7.9 102.4 %all-gather.5.cloned.1.call-start = ((), (), s32[]{:S(2)}) async-start(), calls=%async_computation | async-start | bytes 2228224 | tf_op jit(solution)/shard_map/all_gather | solution.py:36
  8.6 567.1 %all-gather.11.cloned.1.call-start = ((), (), s32[]{:S(2)}) async-start(), calls=%async_computation.3 | async-start | bytes 2228224 | tf_op jit(solution)/shard_map/all_gather | solution.py:35
  140.4 78.7 %collective-permute-start.1 = (f32[64,512]{1,0:T(8,128)S(1)}, f32[64,512]{1,0:T(8,128)S(1)}, u32[]{:S(2)}, u32[]{:S(2)}) collective-permute-start(f32[64,512]{1,0:T(8,128)S(1)} %get-tuple-element.1050), channel_id=1, source_target_pairs={{0,16},{16,32},{32,48},{48,64},{64,80},{80,96},{96,112},{112,128},... | collective-permute-start | bytes 393224 | tf_op jit(solution)/shard_map/while/body/eval_jaxpr/ppermute | solution.py:11
  244.4 11.1 %collective-permute-start.1 = (f32[64,512]{1,0:T(8,128)S(1)}, f32[64,512]{1,0:T(8,128)S(1)}, u32[]{:S(2)}, u32[]{:S(2)}) collective-permute-start(f32[64,512]{1,0:T(8,128)S(1)} %get-tuple-element.1050), channel_id=1, source_target_pairs={{0,16},{16,32},{32,48},{48,64},{64,80},{80,96},{96,112},{112,128},... | collective-permute-start | bytes 393224 | tf_op jit(solution)/shard_map/while/body/eval_jaxpr/ppermute | solution.py:11
  264.4 10.5 collective-permute-start.1
  274.9 10.5 collective-permute-start.1
  285.4 12.3 %collective-permute-start.1 = (f32[64,512]{1,0:T(8,128)S(1)}, f32[64,512]{1,0:T(8,128)S(1)}, u32[]{:S(2)}, u32[]{:S(2)}) collective-permute-start(f32[64,512]{1,0:T(8,128)S(1)} %get-tuple-element.1050), channel_id=1, source_target_pairs={{0,16},{16,32},{32,48},{48,64},{64,80},{80,96},{96,112},{112,128},... | collective-permute-start | bytes 393224 | tf_op jit(solution)/shard_map/while/body/eval_jaxpr/ppermute | solution.py:11
  297.7 11.4 %collective-permute-start.1 = (f32[64,512]{1,0:T(8,128)S(1)}, f32[64,512]{1,0:T(8,128)S(1)}, u32[]{:S(2)}, u32[]{:S(2)}) collective-permute-start(f32[64,512]{1,0:T(8,128)S(1)} %get-tuple-element.1050), channel_id=1, source_target_pairs={{0,16},{16,32},{32,48},{48,64},{64,80},{80,96},{96,112},{112,128},... | collective-permute-start | bytes 393224 | tf_op jit(solution)/shard_map/while/body/eval_jaxpr/ppermute | solution.py:11
  309.2 10.1 collective-permute-start.1
  319.3 11.9 %collective-permute-start.1 = (f32[64,512]{1,0:T(8,128)S(1)}, f32[64,512]{1,0:T(8,128)S(1)}, u32[]{:S(2)}, u32[]{:S(2)}) collective-permute-start(f32[64,512]{1,0:T(8,128)S(1)} %get-tuple-element.1050), channel_id=1, source_target_pairs={{0,16},{16,32},{32,48},{48,64},{64,80},{80,96},{96,112},{112,128},... | collective-permute-start | bytes 393224 | tf_op jit(solution)/shard_map/while/body/eval_jaxpr/ppermute | solution.py:11
  331.3 10.3 collective-permute-start.1
  358.1 15.4 %collective-permute-start = (f32[64,512]{1,0:T(8,128)S(1)}, f32[64,512]{1,0:T(8,128)S(1)}, u32[]{:S(2)}, u32[]{:S(2)}) collective-permute-start(f32[64,512]{1,0:T(8,128)S(1)} %get-tuple-element.1026), channel_id=1, source_target_pairs={{0,1},{1,2},{2,3},{3,4},{4,5},{5,6},{6,7},{7,8},{8,9},{9,10},{10,1... | collective-permute-start | bytes 393224 | tf_op jit(solution)/shard_map/while/body/eval_jaxpr/ppermute | solution.py:11
  543.6 92.6 %all-gather.9.cloned.1.call-start = ((), (), s32[]{:S(2)}) async-start(), calls=%async_computation.2 | async-start | bytes 2228224 | tf_op jit(solution)/shard_map/all_gather | solution.py:36
  666.3 78.7 %collective-permute-start.3 = (f32[64,512]{1,0:T(8,128)S(1)}, f32[64,512]{1,0:T(8,128)S(1)}, u32[]{:S(2)}, u32[]{:S(2)}) collective-permute-start(f32[64,512]{1,0:T(8,128)S(1)} %get-tuple-element.1140), channel_id=1, source_target_pairs={{0,16},{16,32},{32,48},{48,64},{64,80},{80,96},{96,112},{112,128},... | collective-permute-start | bytes 393224 | tf_op jit(solution)/shard_map/while/body/eval_jaxpr/ppermute | solution.py:11
  770.3 11.1 %collective-permute-start.3 = (f32[64,512]{1,0:T(8,128)S(1)}, f32[64,512]{1,0:T(8,128)S(1)}, u32[]{:S(2)}, u32[]{:S(2)}) collective-permute-start(f32[64,512]{1,0:T(8,128)S(1)} %get-tuple-element.1140), channel_id=1, source_target_pairs={{0,16},{16,32},{32,48},{48,64},{64,80},{80,96},{96,112},{112,128},... | collective-permute-start | bytes 393224 | tf_op jit(solution)/shard_map/while/body/eval_jaxpr/ppermute | solution.py:11
  790.3 10.7 collective-permute-start.3
  811.2 12.1 %collective-permute-start.3 = (f32[64,512]{1,0:T(8,128)S(1)}, f32[64,512]{1,0:T(8,128)S(1)}, u32[]{:S(2)}, u32[]{:S(2)}) collective-permute-start(f32[64,512]{1,0:T(8,128)S(1)} %get-tuple-element.1140), channel_id=1, source_target_pairs={{0,16},{16,32},{32,48},{48,64},{64,80},{80,96},{96,112},{112,128},... | collective-permute-start | bytes 393224 | tf_op jit(solution)/shard_map/while/body/eval_jaxpr/ppermute | solution.py:11
  823.4 11.5 %collective-permute-start.3 = (f32[64,512]{1,0:T(8,128)S(1)}, f32[64,512]{1,0:T(8,128)S(1)}, u32[]{:S(2)}, u32[]{:S(2)}) collective-permute-start(f32[64,512]{1,0:T(8,128)S(1)} %get-tuple-element.1140), channel_id=1, source_target_pairs={{0,16},{16,32},{32,48},{48,64},{64,80},{80,96},{96,112},{112,128},... | collective-permute-start | bytes 393224 | tf_op jit(solution)/shard_map/while/body/eval_jaxpr/ppermute | solution.py:11
  834.9 10.2 collective-permute-start.3
  845.2 11.9 %collective-permute-start.3 = (f32[64,512]{1,0:T(8,128)S(1)}, f32[64,512]{1,0:T(8,128)S(1)}, u32[]{:S(2)}, u32[]{:S(2)}) collective-permute-start(f32[64,512]{1,0:T(8,128)S(1)} %get-tuple-element.1140), channel_id=1, source_target_pairs={{0,16},{16,32},{32,48},{48,64},{64,80},{80,96},{96,112},{112,128},... | collective-permute-start | bytes 393224 | tf_op jit(solution)/shard_map/while/body/eval_jaxpr/ppermute | solution.py:11
  867.2 10.7 collective-permute-start.3
  878.0 10.4 collective-permute-start.3
  888.4 11.5 %collective-permute-start.2 = (f32[64,512]{1,0:T(8,128)S(1)}, f32[64,512]{1,0:T(8,128)S(1)}, u32[]{:S(2)}, u32[]{:S(2)}) collective-permute-start(f32[64,512]{1,0:T(8,128)S(1)} %get-tuple-element.1116), channel_id=1, source_target_pairs={{0,1},{1,2},{2,3},{3,4},{4,5},{5,6},{6,7},{7,8},{8,9},{9,10},{10,1... | collective-permute-start | bytes 393224 | tf_op jit(solution)/shard_map/while/body/eval_jaxpr/ppermute | solution.py:11
  (46 other events, 695.5 us)
Sparse Core Ops, SparseCore 0:
  9.8 40.3 all-gather.6
  52.7 57.5 all-gather.4
  543.8 31.9 all-gather.10
  578.6 57.5 all-gather.8
where the time goes:
time: 1080 us
  waiting for transfers between devices  733 us (68%)
  blocking collectives  153 us (14%)
  local copies, waits for them, and re-layouts  121 us (11%)
  matrix products  28.2 us (3%)
  starting transfers between devices  21.7 us (2%)
  between operations  14.7 us (1%)
    ppermute x60, waiting for transfers between devices, passed_along(): lax.ppermute(array, axis, [(i, (i + by) % size) for i in range(size)])  546 us
    all_gather x2, waiting for transfers between devices, expand(): far_vec = lax.all_gather(vectors, 'row', axis=1, tiled=True)  114 us
    dynamic_slice x64, local copies, waits for them, and re-layouts, select_piece(): return lax.dynamic_index_in_dim(pieces, position, 1, keepdims=False)  85.8 us
    psum x1, blocking collectives, on_device(): lax.psum(jnp.stack([cross_term, resid_term, square_term]), ('row', 'col'))  76.6 us
    psum x1, blocking collectives, on_device(): rayleigh = lax.psum(first_term, ('row', 'col')) / total_rows  76.2 us
    all_gather x2, waiting for transfers between devices, expand(): near_vec = lax.all_gather(vectors, 'col', axis=1, tiled=True)  71.1 us
  transfers between devices with their start and end apart: 64, of which 64 were waited for; matrix products, arithmetic and copies ran while one was open for 8% of the time, Pallas kernels for 0%

commit v1 on v0

--- a/solution.py
+++ b/solution.py
@@ -109,7 +109,7 @@
     near_x, far_x, rows_x, cols_x = expand(block)
     image_x = combine_sums(rows_x, cols_x)
     first_term = inner_prod(block, image_x)
-    rayleigh = lax.psum(first_term, ("row", "col")) / total_rows
+    rayleigh = lax.psum(lax.psum(first_term, "row"), "col") / total_rows
     resid = image_x - jnp.dot(
         rayleigh, block, precision=highest, preferred_element_type=jnp.float32
     )

time: 1080 us -> 1130 us (1.046)
  blocking collectives: 153 us -> 208 us
  waiting for transfers between devices: 733 us -> 716 us
  starting transfers between devices: 21.7 us -> 36.7 us
    psum x1 -> x2, blocking collectives: 76.2 us -> 131 us  [on_device(): rayleigh = lax.psum(lax.psum(first_term, 'row'), 'col') / total_rows]
    ppermute x60, waiting for transfers between devices: 546 us -> 530 us  [passed_along(): lax.ppermute(array, axis, [(i, (i + by) % size) for i in range(size)])]
    ppermute x60, starting transfers between devices: 21.6 us -> 36.6 us  [passed_along(): lax.ppermute(array, axis, [(i, (i + by) % size) for i in range(size)])]
where the time goes in v1:
time: 1130 us
  waiting for transfers between devices  716 us (63%)
  blocking collectives  208 us (18%)
  local copies, waits for them, and re-layouts  121 us (11%)
  starting transfers between devices  36.7 us (3%)
  matrix products  28.3 us (3%)
  between operations  14.7 us (1%)
    ppermute x60, waiting for transfers between devices, passed_along(): lax.ppermute(array, axis, [(i, (i + by) % size) for i in range(size)])  530 us
    psum x2, blocking collectives, on_device(): rayleigh = lax.psum(lax.psum(first_term, 'row'), 'col') / total_rows  131 us
    all_gather x2, waiting for transfers between devices, expand(): far_vec = lax.all_gather(vectors, 'row', axis=1, tiled=True)  114 us
    dynamic_slice x64, local copies, waits for them, and re-layouts, select_piece(): return lax.dynamic_index_in_dim(pieces, position, 1, keepdims=False)  85.8 us
    psum x1, blocking collectives, on_device(): lax.psum(jnp.stack([cross_term, resid_term, square_term]), ('row', 'col'))  76.6 us
    all_gather x2, waiting for transfers between devices, expand(): near_vec = lax.all_gather(vectors, 'col', axis=1, tiled=True)  70.4 us
    ppermute x60, starting transfers between devices, passed_along(): lax.ppermute(array, axis, [(i, (i + by) % size) for i in range(size)])  36.6 us
  transfers between devices with their start and end apart: 64, of which 64 were waited for; matrix products, arithmetic and copies ran while one was open for 8% of the time, Pallas kernels for 0%

profile of v1, /device:TPU:1, one launch (start us, length us, event | category | flops | bytes accessed | tf_op | source)
XLA Modules:
  0.0 1130.2 jit_solution(8638603114753900337)
XLA Ops:
  9.4 40.8 %all-gather.7.cloned.1.call-done = f32[64,8192]{1,0:T(8,128)} async-done(((f32[64,512]{1,0:T(8,128)}), f32[64,8192]{1,0:T(8,128)}) %all-gather.7.cloned.1.call-update) | async-done | bytes 2097168 | tf_op jit(solution)/shard_map/all_gather | solution.py:35
  53.4 56.9 %all-gather.5.cloned.1.call-done = f32[64,8192]{1,0:T(8,128)} async-done(((f32[64,512]{1,0:T(8,128)}), f32[64,8192]{1,0:T(8,128)}) %all-gather.5.cloned.1.call-update) | async-done | bytes 2097168 | tf_op jit(solution)/shard_map/all_gather | solution.py:36
  115.4 17.8 %while.84 = (s32[]{:T(128)}, f32[64,32,256]{2,1,0:T(8,128)S(1)}, f32[64,32,256]{2,1,0:T(8,128)}, s32[]{:T(128)}, s32[40]{0:T(128)S(1)}, /*index=5*/s32[40]{0:T(1...) while((s32[]{:T(128)}, f32[64,32,256]{2,1,0:T(8,128)S(1)}, ...), condition=%wide.region_1.3_spmd, body=%wide.region_0.2_spmd.sunk | while | flops 907545280 | bytes 17834760 | solution.py:74
  140.4 212.3 %while.86 = (s32[]{:T(128)}, f32[64,512]{1,0:T(8,128)S(1)}, s32[]{:T(128)}, f32[64,16,512]{2,1,0:T(8,128)}, s32[]{:T(128)}, /*index=5*/s32[]{:T(128)}, s32[]{:T(128)}, s32[]{:T(128)}) while((s32[]{:T(128)}, f32[64,512]{1,0:T(8,128)S(1)}, s32[]{:T(128)}, f32[64,16,512]{2,1,0:T(8,128)}, s32[]{:T(128)}, /*index=5*/s32[]{:T(128)}, s32[]{:T(128)}, ...), condition=%wide.region_5.7_spmd, body=%wide.region_4.6_spmd.sunk | while | flops 32785 | bytes 1179932 | solution.py:106
  143.3 75.1 %collective-permute-done.1 = f32[64,512]{1,0:T(8,128)S(1)} collective-permute-done((f32[64,512]{1,0:T(8,128)S(1)}, f32[64,512]{1,0:T(8,128)S(1)}, u32[]{:S(2)}, u32[]{:S(2)}) %collective-permute-start.1) | collective-permute-done | bytes 131104 | tf_op jit(solution)/shard_map/while/body/eval_jaxpr/ppermute | solution.py:11
  245.7 9.9 collective-permute-done.1
  310.4 9.8 collective-permute-done.1
  321.7 9.7 collective-permute-done.1
  332.9 9.5 collective-permute-done.1
  352.7 113.7 %while.85 = (s32[]{:T(128)}, f32[64,512]{1,0:T(8,128)S(1)}, s32[]{:T(128)}, f32[64,16,512]{2,1,0:T(8,128)}, s32[]{:T(128)}, /*index=5*/s32[]{:T(128)}, s32[]{:T(128)}, s32[]{:T(128)}) while((s32[]{:T(128)}, f32[64,512]{1,0:T(8,128)S(1)}, s32[]{:T(128)}, f32[64,16,512]{2,1,0:T(8,128)}, s32[]{:T(128)}, /*index=5*/s32[]{:T(128)}, s32[]{:T(128)}, ...), condition=%wide.region_3.5_spmd, body=%wide.region_2.4_spmd.sunk | while | flops 32785 | bytes 1179932 | solution.py:105
  352.7 14.8 %collective-permute-start = (f32[64,512]{1,0:T(8,128)S(1)}, f32[64,512]{1,0:T(8,128)S(1)}, u32[]{:S(2)}, u32[]{:S(2)}) collective-permute-start(f32[64,512]{1,0:T(8,128)S(1)} %get-tuple-element.1026), channel_id=1, source_target_pairs={{0,1},{1,2},{2,3},{3,4},{4,5},{5,6},{6,7},{7,8},{8,9},{9,10},{10,1... | collective-permute-start | bytes 393224 | tf_op jit(solution)/shard_map/while/body/eval_jaxpr/ppermute | solution.py:11
  466.7 63.3 %psum.21 = f32[64,64]{0,1:T(8,128)S(1)} all-reduce(f32[64,64]{0,1:T(8,128)S(1)} %convolution_bitcast_fusion.3), channel_id=1, replica_groups=mesh['row'=16,'col'=16] {'row'}, use_global_device_ids=true, to_apply=%region_6.8 | all-reduce | flops 4096 | bytes 32768 | tf_op jit(solution)/shard_map/psum | solution.py:112
  530.0 67.7 %psum.22 = f32[64,64]{0,1:T(8,128)S(1)} all-reduce(f32[64,64]{0,1:T(8,128)S(1)} %psum.21), channel_id=1, replica_groups=mesh['row'=16,'col'=16] {'col'}, use_global_device_ids=true, to_apply=%region_7.9 | all-reduce | flops 4096 | bytes 32768 | tf_op jit(solution)/shard_map/psum | solution.py:112
  600.6 29.6 %all-gather.11.cloned.1.call-done = f32[64,8192]{1,0:T(8,128)} async-done(((f32[64,512]{1,0:T(8,128)}), f32[64,8192]{1,0:T(8,128)}) %all-gather.11.cloned.1.call-update) | async-done | bytes 2097168 | tf_op jit(solution)/shard_map/all_gather | solution.py:35
  633.4 57.3 %all-gather.9.cloned.1.call-done = f32[64,8192]{1,0:T(8,128)} async-done(((f32[64,512]{1,0:T(8,128)}), f32[64,8192]{1,0:T(8,128)}) %all-gather.9.cloned.1.call-update) | async-done | bytes 2097168 | tf_op jit(solution)/shard_map/all_gather | solution.py:36
  695.8 17.8 %while.87 = (s32[]{:T(128)}, f32[64,32,256]{2,1,0:T(8,128)S(1)}, f32[64,32,256]{2,1,0:T(8,128)}, s32[]{:T(128)}, s32[40]{0:T(128)S(1)}, /*index=5*/s32[40]{0:T(1...) while((s32[]{:T(128)}, f32[64,32,256]{2,1,0:T(8,128)S(1)}, ...), condition=%wide.region_9.11_spmd, body=%wide.region_8.10_spmd.sunk | while | flops 907545280 | bytes 17834760 | solution.py:74
  720.8 212.2 %while.89 = (s32[]{:T(128)}, f32[64,512]{1,0:T(8,128)S(1)}, s32[]{:T(128)}, f32[64,16,512]{2,1,0:T(8,128)}, s32[]{:T(128)}, /*index=5*/s32[]{:T(128)}, s32[]{:T(128)}, s32[]{:T(128)}) while((s32[]{:T(128)}, f32[64,512]{1,0:T(8,128)S(1)}, s32[]{:T(128)}, f32[64,16,512]{2,1,0:T(8,128)}, s32[]{:T(128)}, /*index=5*/s32[]{:T(128)}, s32[]{:T(128)}, ...), condition=%wide.region_13.15_spmd, body=%wide.region_12.14_spmd.sunk | while | flops 32785 | bytes 1179932 | solution.py:106
  723.7 75.1 %collective-permute-done.3 = f32[64,512]{1,0:T(8,128)S(1)} collective-permute-done((f32[64,512]{1,0:T(8,128)S(1)}, f32[64,512]{1,0:T(8,128)S(1)}, u32[]{:S(2)}, u32[]{:S(2)}) %collective-permute-start.3) | collective-permute-done | bytes 131104 | tf_op jit(solution)/shard_map/while/body/eval_jaxpr/ppermute | solution.py:11
  826.3 9.5 collective-permute-done.3
  847.6 9.4 collective-permute-done.3
  868.3 10.6 collective-permute-done.3
  933.0 112.6 %while.88 = (s32[]{:T(128)}, f32[64,512]{1,0:T(8,128)S(1)}, s32[]{:T(128)}, f32[64,16,512]{2,1,0:T(8,128)}, s32[]{:T(128)}, /*index=5*/s32[]{:T(128)}, s32[]{:T(128)}, s32[]{:T(128)}) while((s32[]{:T(128)}, f32[64,512]{1,0:T(8,128)S(1)}, s32[]{:T(128)}, f32[64,16,512]{2,1,0:T(8,128)}, s32[]{:T(128)}, /*index=5*/s32[]{:T(128)}, s32[]{:T(128)}, ...), condition=%wide.region_11.13_spmd, body=%wide.region_10.12_spmd.sunk | while | flops 32785 | bytes 1179932 | solution.py:105
  933.0 13.9 %collective-permute-start.2 = (f32[64,512]{1,0:T(8,128)S(1)}, f32[64,512]{1,0:T(8,128)S(1)}, u32[]{:S(2)}, u32[]{:S(2)}) collective-permute-start(f32[64,512]{1,0:T(8,128)S(1)} %get-tuple-element.1116), channel_id=1, source_target_pairs={{0,1},{1,2},{2,3},{3,4},{4,5},{5,6},{6,7},{7,8},{8,9},{9,10},{10,1... | collective-permute-start | bytes 393224 | tf_op jit(solution)/shard_map/while/body/eval_jaxpr/ppermute | solution.py:11
  1046.3 76.6 %psum.23 = f32[3,64,64]{1,2,0:T(8,128)S(1)} all-reduce(f32[3,64,64]{1,2,0:T(8,128)S(1)} %pad_maximum_fusion.1), channel_id=1, replica_groups=mesh['row'=16,'col'=16] {'row','col'}, use_global_device_ids=true, to_apply=%region_14.16 | all-reduce | flops 12288 | bytes 98304 | tf_op jit(solution)/shard_map/psum | solution.py:121
  (305 shorter events, 472.8 us)
Async XLA Ops:
  7.2 43.1 %all-gather.7.cloned.1.call-start = ((), (), s32[]{:S(2)}) async-start(), calls=%async_computation.1 | async-start | bytes 2228224 | tf_op jit(solution)/shard_map/all_gather | solution.py:35
  7.9 102.4 %all-gather.5.cloned.1.call-start = ((), (), s32[]{:S(2)}) async-start(), calls=%async_computation | async-start | bytes 2228224 | tf_op jit(solution)/shard_map/all_gather | solution.py:36
  8.6 621.6 %all-gather.11.cloned.1.call-start = ((), (), s32[]{:S(2)}) async-start(), calls=%async_computation.3 | async-start | bytes 2228224 | tf_op jit(solution)/shard_map/all_gather | solution.py:35
  140.4 78.0 %collective-permute-start.1 = (f32[64,512]{1,0:T(8,128)S(1)}, f32[64,512]{1,0:T(8,128)S(1)}, u32[]{:S(2)}, u32[]{:S(2)}) collective-permute-start(f32[64,512]{1,0:T(8,128)S(1)} %get-tuple-element.1050), channel_id=1, source_target_pairs={{0,16},{16,32},{32,48},{48,64},{64,80},{80,96},{96,112},{112,128},... | collective-permute-start | bytes 393224 | tf_op jit(solution)/shard_map/while/body/eval_jaxpr/ppermute | solution.py:11
  235.4 8.9 collective-permute-start.1
  244.2 11.4 %collective-permute-start.1 = (f32[64,512]{1,0:T(8,128)S(1)}, f32[64,512]{1,0:T(8,128)S(1)}, u32[]{:S(2)}, u32[]{:S(2)}) collective-permute-start(f32[64,512]{1,0:T(8,128)S(1)} %get-tuple-element.1050), channel_id=1, source_target_pairs={{0,16},{16,32},{32,48},{48,64},{64,80},{80,96},{96,112},{112,128},... | collective-permute-start | bytes 393224 | tf_op jit(solution)/shard_map/while/body/eval_jaxpr/ppermute | solution.py:11
  289.0 10.1 collective-permute-start.1
  299.1 9.8 collective-permute-start.1
  308.9 11.3 collective-permute-start.1
  320.2 11.2 collective-permute-start.1
  331.4 11.0 collective-permute-start.1
  342.5 10.1 collective-permute-start.1
  352.7 21.1 %collective-permute-start = (f32[64,512]{1,0:T(8,128)S(1)}, f32[64,512]{1,0:T(8,128)S(1)}, u32[]{:S(2)}, u32[]{:S(2)}) collective-permute-start(f32[64,512]{1,0:T(8,128)S(1)} %get-tuple-element.1026), channel_id=1, source_target_pairs={{0,1},{1,2},{2,3},{3,4},{4,5},{5,6},{6,7},{7,8},{8,9},{9,10},{10,1... | collective-permute-start | bytes 393224 | tf_op jit(solution)/shard_map/while/body/eval_jaxpr/ppermute | solution.py:11
  598.8 92.0 %all-gather.9.cloned.1.call-start = ((), (), s32[]{:S(2)}) async-start(), calls=%async_computation.2 | async-start | bytes 2228224 | tf_op jit(solution)/shard_map/all_gather | solution.py:36
  720.8 78.0 %collective-permute-start.3 = (f32[64,512]{1,0:T(8,128)S(1)}, f32[64,512]{1,0:T(8,128)S(1)}, u32[]{:S(2)}, u32[]{:S(2)}) collective-permute-start(f32[64,512]{1,0:T(8,128)S(1)} %get-tuple-element.1140), channel_id=1, source_target_pairs={{0,16},{16,32},{32,48},{48,64},{64,80},{80,96},{96,112},{112,128},... | collective-permute-start | bytes 393224 | tf_op jit(solution)/shard_map/while/body/eval_jaxpr/ppermute | solution.py:11
  815.7 9.1 collective-permute-start.3
  824.8 11.0 collective-permute-start.3
  835.9 10.3 collective-permute-start.3
  846.2 10.8 collective-permute-start.3
  857.0 9.8 collective-permute-start.3
  866.9 12.1 %collective-permute-start.3 = (f32[64,512]{1,0:T(8,128)S(1)}, f32[64,512]{1,0:T(8,128)S(1)}, u32[]{:S(2)}, u32[]{:S(2)}) collective-permute-start(f32[64,512]{1,0:T(8,128)S(1)} %get-tuple-element.1140), channel_id=1, source_target_pairs={{0,16},{16,32},{32,48},{48,64},{64,80},{80,96},{96,112},{112,128},... | collective-permute-start | bytes 393224 | tf_op jit(solution)/shard_map/while/body/eval_jaxpr/ppermute | solution.py:11
  879.0 10.8 collective-permute-start.3
  922.9 10.1 collective-permute-start.3
  933.0 20.0 %collective-permute-start.2 = (f32[64,512]{1,0:T(8,128)S(1)}, f32[64,512]{1,0:T(8,128)S(1)}, u32[]{:S(2)}, u32[]{:S(2)}) collective-permute-start(f32[64,512]{1,0:T(8,128)S(1)} %get-tuple-element.1116), channel_id=1, source_target_pairs={{0,1},{1,2},{2,3},{3,4},{4,5},{5,6},{6,7},{7,8},{8,9},{9,10},{10,1... | collective-permute-start | bytes 393224 | tf_op jit(solution)/shard_map/while/body/eval_jaxpr/ppermute | solution.py:11
  (46 other events, 759.2 us)
Sparse Core Ops, SparseCore 0:
  9.8 40.3 all-gather.6
  52.7 57.5 all-gather.4
  598.9 31.2 all-gather.10
  633.2 57.5 all-gather.8
